TPU v7x, 128 devices: a whole 4x4x4 slice. The times are simulated.
128 devices in a mesh: ctx: 32 (over y, z, core), exp: 4 (over x).
Axes of the slice: x: 4, y: 4, z: 4, core: 2. Of those that a mesh axis runs over, the one named last changes fastest.
Arguments:
- inputs: bfloat16 [4096, 4096], P('ctx', 'exp'), may hold values from -6 to 6
- gate_input: bfloat16 [4096, 4096], P('ctx', 'exp')
- b_proj: bfloat16 [4096, 128], P('ctx'), may hold values from -0.5 to 0.5
- c_proj: bfloat16 [4096, 128], P('ctx'), may hold values from -6 to 6
- step_size: float32 [64, 4096], P('exp', 'ctx'), may hold values from 0.03 to 0.3
- decay_rate: float32 [64, 4096], P('exp', 'ctx'), as said below
- skip_gain: float32 [64], P('exp'), may hold values from 0.5 to 2
- start_state: float32 [64, 64, 128], P('exp'), may hold values from -3 to 3
- norm_gain: float32 [4096], P('exp'), may hold values from 0.5 to 1.5
- out_proj: bfloat16 [4096, 4096], P('exp', 'ctx'), may hold values from -0.09375 to 0.09375
- residual: bfloat16 [4096, 4096], P('ctx'), may hold values from -6 to 6
- moe_gain: float32 [4096], replicated, may hold values from 0.5 to 1.5
- w_gate: bfloat16 [32, 4096, 3584], P('ctx', None, 'exp'), may hold values from -0.09375 to 0.09375
- w_up: bfloat16 [32, 4096, 3584], P('ctx', None, 'exp'), may hold values from -0.09375 to 0.09375
- w_down: bfloat16 [32, 3584, 4096], P('ctx', 'exp'), may hold values from -0.0625 to 0.0625
- route_ids: int32 [4096, 2], P('ctx'), may hold values from 0 to 15, all different within a row; in each aligned block of 32 rows (0 to 31, 32 to 63, ...) at most 8 rows name the same one
- route_gates: float32 [4096, 2], P('ctx'), may hold values from 0.3 to 1
Outputs:
- output: bfloat16 [4096, 4096], P(('ctx', 'exp'))
Inputs may be any that keep to these rules, and one draw needn't show every extreme that they name: `route_ids`: each row names two different experts. In each aligned block of 32 rows no expert is named more than 8 times, a bound that some block reaches. `decay_rate`: Non-negative.
All inputs are finite; a program needn't handle non-finite values.
Results may differ from a plain program's by a relative error of at most 0.02.
Values may be sent and summed in bfloat16 or wider, within the bound.
A program may use at most 128 MiB of HBM per device.

v0:
```python
import jax
import jax.numpy as jnp
from jax import lax
from jax.sharding import PartitionSpec as P

PAIR = 2
eps_norm = 1e-05
top_precision = lax.Precision.HIGHEST


def entering(x, axis, join, neutral):
    place = lax.axis_index(axis)
    gathered = jax.tree.map(
        lambda a, kind: lax.all_gather(a.astype(kind), axis), x, (jnp.bfloat16, jnp.bfloat16)
    )
    state = jax.tree.map(lambda a, e: jnp.zeros_like(a) + jnp.asarray(e, a.dtype), x, neutral)

    def one(hop, state):
        return join(
            state,
            jax.tree.map(
                lambda a, own: lax.dynamic_index_in_dim(a, hop, 0, False).astype(own.dtype),
                gathered,
                x,
            ),
        )

    return lax.fori_loop(0, place, one, state)


def later_state(earlier, later):
    first_decay, first_state = earlier
    second_decay, second_state = later
    return (first_decay * second_decay, second_decay[:, None, None] * first_state + second_state)


def route_ranks(quarter_ids, experts):
    flattened = quarter_ids.reshape(-1)
    onehot = (flattened[:, None] == jnp.arange(experts, dtype=jnp.int32)[None, :]).astype(jnp.int32)
    running = jnp.cumsum(onehot, axis=0)
    rank_ids = jnp.sum(onehot * running, axis=1) - 1
    return (flattened, rank_ids)


def place_rows(normed, quarter_ids, experts, capacity):
    flattened, rank_ids = route_ranks(quarter_ids, experts)
    slot_ids = rank_ids * experts + flattened
    matches = (
        jnp.arange(capacity * experts, dtype=jnp.int32)[:, None] == slot_ids[None, :]
    ).astype(jnp.bfloat16)
    doubled = jnp.repeat(normed, quarter_ids.shape[1], axis=0)
    placed = jnp.dot(matches, doubled, preferred_element_type=jnp.float32).astype(jnp.bfloat16)
    return placed.reshape(capacity, experts, normed.shape[1])


def rms_rows(values, gain_vec):
    scaling = lax.rsqrt(jnp.mean(values * values, axis=1, keepdims=True) + eps_norm)
    return (values * scaling * gain_vec[None, :]).astype(jnp.bfloat16)


def local(
    inputs,
    gate_input,
    b_proj,
    c_proj,
    step_size,
    decay_rate,
    skip_gain,
    start_state,
    norm_gain,
    out_proj,
    residual,
    moe_gain,
    w_gate,
    w_up,
    w_down,
    route_ids,
    route_gates,
):
    tok_ctx = inputs.shape[0]
    head_count = step_size.shape[0]
    head_dim = inputs.shape[1] // head_count
    model_width = residual.shape[1]
    n_ctx = lax.axis_size("ctx")
    n_exp = lax.axis_size("exp")
    experts = n_ctx // PAIR
    tok_quarter = tok_ctx // n_exp
    capacity = 4 * tok_quarter // experts
    x_local = inputs.astype(jnp.float32).reshape(tok_ctx, head_count, head_dim)
    b_local = b_proj.astype(jnp.float32)
    c_local = c_proj.astype(jnp.float32)
    cumulative = jnp.cumsum(decay_rate, axis=1)
    span_total = cumulative[:, -1]
    sequence_indices = jnp.arange(tok_ctx, dtype=jnp.int32)
    causal = sequence_indices[:, None] >= sequence_indices[None, :]
    spread = jnp.where(causal[None], cumulative[:, :, None] - cumulative[:, None, :], 0.0)
    scores = jnp.dot(c_local, b_local.T, precision=top_precision)
    mixing = jnp.where(causal[None], jnp.exp(-spread), 0.0) * scores[None] * step_size[:, None, :]
    inside_part = jnp.einsum("hts,shp->thp", mixing, x_local, precision=top_precision)
    ending = jnp.exp(-(span_total[:, None] - cumulative)) * step_size
    local_state = jnp.einsum("hs,shp,sn->hpn", ending, x_local, b_local, precision=top_precision)
    prior_decay, prior_state = entering(
        (jnp.exp(-span_total), local_state),
        "ctx",
        later_state,
        (jnp.ones_like(span_total), jnp.zeros_like(local_state)),
    )
    incoming = prior_state + prior_decay[:, None, None] * start_state
    carried = (
        jnp.einsum("hpn,tn->thp", incoming, c_local, precision=top_precision)
        * jnp.exp(-cumulative).T[:, :, None]
    )
    ssm_out = inside_part + carried + skip_gain[None, :, None] * x_local
    gated_out = ssm_out.reshape(tok_ctx, head_count * head_dim) * jax.nn.silu(
        gate_input.astype(jnp.float32)
    )
    squares = lax.psum(jnp.sum(gated_out * gated_out, axis=1), "exp")
    scaling = lax.rsqrt(squares / (head_count * head_dim * n_exp) + eps_norm)
    normed_mix = (gated_out * scaling[:, None] * norm_gain[None, :]).astype(jnp.bfloat16)
    partial_value = jnp.dot(
        normed_mix,
        lax.all_gather(out_proj, "ctx", axis=1, tiled=True),
        preferred_element_type=jnp.float32,
    )
    gate_rows = w_gate[0]
    up_rows = w_up[0]
    down_rows = w_down[0]
    piece_width = gate_rows.shape[1]
    first_row = lax.axis_index("exp") * tok_quarter
    own_ids = lax.dynamic_slice_in_dim(route_ids, first_row, tok_quarter, 0)
    own_gates = lax.dynamic_slice_in_dim(route_gates, first_row, tok_quarter, 0)
    mixed_all = lax.psum(partial_value.astype(jnp.bfloat16), "exp").astype(jnp.float32)
    hidden_all = residual.astype(jnp.float32) + mixed_all
    moe_all = rms_rows(hidden_all, moe_gain)

    def place_quarter(quarter_rows, quarter_ids):
        return place_rows(quarter_rows, quarter_ids, experts, capacity)

    placed = jax.vmap(place_quarter)(
        moe_all.reshape(n_exp, tok_quarter, model_width),
        route_ids.reshape(n_exp, tok_quarter, route_ids.shape[1]),
    )
    placed = placed.reshape(n_exp * capacity, experts, model_width)
    outgoing = jnp.repeat(placed, PAIR, axis=1)
    arrived = lax.all_to_all(outgoing, "ctx", split_axis=1, concat_axis=1, tiled=True)
    flattened = arrived.reshape(-1, model_width)
    gate_val = jnp.dot(flattened, gate_rows, preferred_element_type=jnp.float32)
    up_val = jnp.dot(flattened, up_rows, preferred_element_type=jnp.float32)
    activated = (jax.nn.silu(gate_val) * up_val).astype(jnp.bfloat16)
    hidden = activated.reshape(arrived.shape[0], arrived.shape[1], piece_width)
    hidden_own = lax.dynamic_slice_in_dim(hidden_all, first_row, tok_quarter, 0)
    product = jnp.dot(
        hidden.reshape(-1, piece_width), down_rows, preferred_element_type=jnp.float32
    )
    rounded = lax.optimization_barrier(product.astype(jnp.bfloat16)).astype(jnp.float32)
    summed = lax.psum_scatter(
        rounded.reshape(lax.axis_size("exp") * capacity, hidden.shape[1], model_width).astype(
            jnp.bfloat16
        ),
        "exp",
        scatter_dimension=0,
        tiled=True,
    )
    halves = lax.all_to_all(summed, "ctx", split_axis=1, concat_axis=1, tiled=True)
    flattened, rank_ids = route_ranks(own_ids, experts)
    base_rows = rank_ids * n_ctx + flattened * PAIR
    fetch_rows = base_rows[:, None] + jnp.arange(PAIR, dtype=jnp.int32)[None, :]
    fetched = halves.reshape(capacity * n_ctx, model_width)[fetch_rows]
    expert_out = jnp.sum(fetched.astype(jnp.float32), axis=1)
    weighted = expert_out * own_gates.reshape(-1)[:, None]
    moe_out = jnp.sum(weighted.reshape(tok_quarter, -1, model_width), axis=1)
    return (hidden_own + moe_out).astype(jnp.bfloat16)


def solution(mesh):
    in_specs = (
        P("ctx", "exp"),
        P("ctx", "exp"),
        P("ctx", None),
        P("ctx", None),
        P("exp", "ctx"),
        P("exp", "ctx"),
        P("exp"),
        P("exp", None, None),
        P("exp"),
        P("exp", "ctx"),
        P("ctx", None),
        P(),
        P("ctx", None, "exp"),
        P("ctx", None, "exp"),
        P("ctx", "exp", None),
        P("ctx", None),
        P("ctx", None),
    )
    out_specs = P(("ctx", "exp"), None)
    return jax.shard_map(local, mesh=mesh, in_specs=in_specs, out_specs=out_specs, check_vma=False)
```

profile of v0, /device:TPU:1, one launch (start us, length us, event | category | flops | bytes accessed | tf_op | source)
XLA Modules:
  0.0 490.3 jit_solution(6920894452097007620)
XLA Ops:
  6.5 1.0 reduce_window_sum.33
  7.5 0.2 slice_reduce_fusion
  7.7 1.1 copy.61
  8.8 0.8 exponential_bitcast_fusion
  9.6 1.1 convolution_convert_fusion.3
  10.7 0.0 all-gather.5.cloned.1.call-start
  10.8 0.7 all-gather.5.cloned.1.call-update
  11.5 0.0 all-reduce.3.cloned.1.call-start
  11.6 1.2 dynamic-slice
  13.4 0.2 fusion.38
  13.6 0.2 dynamic-update-slice
  13.8 65.5 %all-reduce = bf16[512]{0:T(512)(128)(2,1)S(1)} all-reduce(bf16[512]{0:T(512)(128)(2,1)S(1)} %dynamic-update-slice), channel_id=2, replica_groups=mesh['ctx'=32,'exp'=4] {'ctx'}, use_global_device_ids=true, to_apply=%add | all-reduce | flops 512 | bytes 2048
  79.3 0.1 reshape.172
  79.5 0.9 fusion.42
  80.3 0.0 copy-start.7
  80.5 1.2 while.12
  80.5 1.1 convert_add_fusion.3
  81.7 0.5 fusion.9
  82.2 1.4 fusion.8
  83.6 0.2 copy.62
  83.8 0.2 multiply_reduce_fusion.2
  84.1 8.4 %psum.14 = f32[128]{0:T(128)S(1)} all-reduce(f32[128]{0:T(128)S(1)} %multiply_reduce_fusion.2), channel_id=1, replica_groups=mesh['ctx'=32,'exp'=4] {'exp'}, use_global_device_ids=true, to_apply=%region_4.5 | all-reduce | flops 128 | bytes 1024 | tf_op jit(solution)/shard_map/psum | solution.py:117
  92.5 36.7 %all-gather.5.cloned.1.call-done = bf16[1024,4096]{1,0:T(8,128)(2,1)} async-done(((bf16[1024,128]{1,0:T(8,128)(2,1)}), bf16[1024,4096]{1,0:T(8,128)(2,1)}) %all-gather.5.cloned.1.call-update) | async-done | bytes 8388624 | tf_op jit(solution)/shard_map/all_gather | solution.py:122
  129.2 5.8 %convolution_convert_fusion.2 = bf16[128,4096]{1,0:T(8,128)(2,1)} fusion(bf16[1024,4096]{1,0:T(8,128)(2,1)} %all-gather.5.cloned.1.call-done, f32[1024]{0:T(1024)S(1)} %copy-done.12, f32[128]{0:T(128)S(1)} %add_rsqrt_fusion.1, f32[128,1024]{1,0:T(8,128)S(1)} %copy.62, bf16[128,1024]{1,0:T(8,128)(2,1)S(1)} %copy-done.6), kind=kOutput, calls=%fused_computation.10 | convolution fusion | flops 1075445760 | bytes 10228224 | tf_op jit(solution)/shard_map/dot_general | solution.py:120
  135.1 0.0 reduce-scatter.4.cloned.1.call-start
  135.1 0.1 copy.63
  135.2 0.1 eq.44
  135.3 0.1 fusion.33
  135.5 0.1 reduce_window_sum.34
  135.6 0.2 select_reduce_fusion
  135.8 42.9 %all-reduce.3.cloned.1.call-done = bf16[128,4096]{1,0:T(8,128)(2,1)} async-done(((bf16[128,4096]{1,0:T(8,128)(2,1)}), bf16[128,4096]{1,0:T(8,128)(2,1)}) %all-reduce.3.cloned.1.call-update) | async-done | bytes 1048592 | tf_op jit(solution)/shard_map/psum | solution.py:132
  178.8 3.0 convert_add_fusion.1
  181.8 0.4 multiply_convert_fusion.1
  182.2 3.4 broadcast_in_dim.28
  185.7 2.7 reshape.157
  188.4 1.4 convolution_convert_fusion.1
  189.8 2.3 copy.64
  192.1 4.3 broadcast_in_dim.29
  196.3 105.0 %all_to_all.10 = bf16[32,32,4096]{2,0,1:T(8,128)(2,1)} all-to-all(bf16[32,32,4096]{2,0,1:T(8,128)(2,1)} %bitcast.66), channel_id=1, replica_groups=mesh['ctx'=32,'exp'=4] {'ctx'}, dimensions={1} | all-to-all | bytes 16777216 | tf_op jit(solution)/shard_map/all_to_all | solution.py:145
  301.4 11.3 %copy.65 = bf16[32,32,4096]{2,1,0:T(8,128)(2,1)} copy(bf16[32,32,4096]{2,0,1:T(8,128)(2,1)} %all_to_all.10) | data formatting | bytes 16777216 | tf_op jit(solution)/shard_map/all_to_all | solution.py:145
  312.7 13.0 %fusion.1 = f32[1024,896]{1,0:T(8,128)S(1)} fusion(bf16[1024,4096]{1,0:T(8,128)(2,1)} %bitcast.68, bf16[1,4096,896]{2,1,0:T(8,128)(2,1)} %param.32), kind=kOutput, calls=%fused_computation.5 | convolution fusion | flops 7516192768 | bytes 19398656 | tf_op jit(solution)/shard_map/dot_general | solution.py:148
  325.8 9.2 %multiply_convert_fusion = bf16[1024,896]{1,0:T(8,128)(2,1)S(1)} fusion(f32[1024,896]{1,0:T(8,128)S(1)} %fusion.1, bf16[1024,4096]{1,0:T(8,128)(2,1)S(1)} %bitcast.69, bf16[1,4096,896]{2,1,0:T(8,128)(2,1)S(1)} %bitcast.78), kind=kOutput, calls=%fused_computation.11 | convolution fusion | flops 7521697792 | bytes 21233664 | tf_op jit(solution)/shard_map/dot_general | solution.py:147
  335.0 11.2 %convolution_convert_fusion = bf16[1024,4096]{1,0:T(8,128)(2,1)} fusion(bf16[1024,896]{1,0:T(8,128)(2,1)S(1)} %multiply_convert_fusion, bf16[1,896,4096]{2,1,0:T(8,128)(2,1)S(1)} %bitcast.80), kind=kOutput, calls=%fused_computation.3 | convolution fusion | flops 7520387072 | bytes 17563648 | tf_op jit(solution)/shard_map/dot_general | solution.py:152
  346.2 11.3 %copy.74 = bf16[4,8,32,4096]{3,1,2,0:T(8,128)(2,1)} copy(bf16[4,8,32,4096]{3,2,1,0:T(8,128)(2,1)} %bitcast.70) | data formatting | bytes 16777216
  357.5 77.8 %reduce-scatter.4.cloned.1.call-done = bf16[8,131072]{1,0:T(8,128)(2,1)} async-done(((bf16[32,131072]{1,0:T(8,128)(2,1)}), bf16[8,131072]{1,0:T(8,128)(2,1)}) %reduce-scatter.4.cloned.1.call-update) | async-done | bytes 2097168
  435.3 8.1 %all-to-all-start.1 = ((bf16[8,32,4096]{2,0,1:T(8,128)(2,1)}), bf16[8,32,4096]{2,0,1:T(8,128)(2,1)}, u32[]{:S(2)}, u32[]{:S(2)}) async-start(bf16[8,32,4096]{2,0,1:T(8,128)(2,1)} %bitcast.72), calls=%async_computation.1 | async-start | bytes 4194304 | tf_op jit(solution)/shard_map/all_to_all | solution.py:164
  443.4 0.1 constant_dynamic-slice_fusion
  443.5 0.1 copy.68
  443.6 0.1 eq.50
  443.7 0.1 fusion.37
  443.8 0.1 reduce_window_sum.35
  443.9 0.2 select_reduce_fusion.1
  444.1 0.1 compare_select_fusion
  444.2 0.1 reshape.166
  444.3 0.1 constant_dynamic-slice_fusion.1
  444.4 0.1 copy.69
  444.5 27.1 %all-to-all-done.1 = bf16[8,32,4096]{2,0,1:T(8,128)(2,1)} async-done(((bf16[8,32,4096]{2,0,1:T(8,128)(2,1)}), bf16[8,32,4096]{2,0,1:T(8,128)(2,1)}, u32[]{:S(2)}, u32[]{:S(2)}) %all-to-all-start.1) | async-done | bytes 2097184 | tf_op jit(solution)/shard_map/all_to_all | solution.py:164
  471.6 2.7 copy.67
  474.3 1.2 gather_fusion
  475.5 1.3 reshape.175
  476.9 2.7 reduce_sum.60
  479.6 0.6 reduce_sum.61
  480.2 1.4 multiply_reduce_fusion.1
  481.7 1.8 add_convert_fusion
  (52 shorter events, 0.3 us)
Async XLA Ops:
  6.5 3.1 copy-start
  6.5 73.9 %all-gather.7.cloned.1.call-start = ((), (), s32[]{:S(2)}) async-start(), calls=%async_computation.5 | async-start | bytes 8650752 | tf_op jit(solution)/shard_map/all_gather | solution.py:14
  10.7 118.4 %all-gather.5.cloned.1.call-start = ((), (), s32[]{:S(2)}) async-start(), calls=%async_computation.3 | async-start | bytes 8650752 | tf_op jit(solution)/shard_map/all_gather | solution.py:122
  11.5 167.3 %all-reduce.3.cloned.1.call-start = ((), (), s32[]{:S(2)}) async-start(), calls=%async_computation.4 | async-start | bytes 2097152 | tf_op jit(solution)/shard_map/psum | solution.py:132
  80.3 1.4 copy-start.5
  80.3 1.4 copy-start.7
  80.5 1.7 copy-start.9
  80.5 1.7 copy-start.13
  81.7 2.1 copy-start.6
  81.7 47.5 %copy-start.12 = (f32[1024]{0:T(1024)S(1)}, f32[1024]{0:T(1024)}, u32[]{:S(2)}) copy-start(f32[1024]{0:T(1024)} %param.27) | copy-start | bytes 12292
  92.5 42.6 %copy-start.10 = (s32[128,2]{0,1:T(2,128)S(1)}, s32[128,2]{0,1:T(2,128)}, u32[]{:S(2)}) copy-start(s32[128,2]{0,1:T(2,128)} %param.34) | copy-start | bytes 3076
  92.5 86.3 %copy-start.3 = (bf16[128,4096]{1,0:T(8,128)(2,1)S(1)}, bf16[128,4096]{1,0:T(8,128)(2,1)}, u32[]{:S(2)}) copy-start(bf16[128,4096]{1,0:T(8,128)(2,1)} %param.29) | copy-start | bytes 3145732
  135.0 46.8 %copy-start.8 = (f32[4096]{0:T(1024)S(1)}, f32[4096]{0:T(1024)}, u32[]{:S(2)}) copy-start(f32[4096]{0:T(1024)} %param.30) | copy-start | bytes 49156
  135.1 300.3 %reduce-scatter.4.cloned.1.call-start = ((), (), s32[]{:S(2)}) async-start(), calls=%async_computation.6 | async-start | bytes 10485760
  178.8 3.0 copy-start.4
  301.4 24.4 %slice-start = ((s8[7340032]{0:T(1024)(128)(4,1)}), s8[3145728]{0:T(1024)(128)(4,1)S(1)}, s32[]{:S(2)}) async-start(s8[7340032]{0:T(1024)(128)(4,1)} %bitcast.77), calls=%async_computation.7 | async-start | bytes 6291456
  312.7 13.0 %copy-start.2 = (bf16[32,32,4096]{2,1,0:T(8,128)(2,1)S(1)}, bf16[32,32,4096]{2,1,0:T(8,128)(2,1)}, u32[]{:S(2)}) copy-start(bf16[32,32,4096]{2,1,0:T(8,128)(2,1)} %copy.65) | copy-start | bytes 25165828
  312.7 13.0 %slice-start.1 = ((s8[7340032]{0:T(1024)(128)(4,1)}), s8[4194304]{0:T(1024)(128)(4,1)S(1)}, s32[]{:S(2)}) async-start(s8[7340032]{0:T(1024)(128)(4,1)} %bitcast.77), calls=%async_computation.8 | async-start | bytes 8388608
  312.7 22.2 %slice-start.2 = ((s8[7340032]{0:T(1024)(128)(4,1)}), s8[4194304]{0:T(1024)(128)(4,1)S(1)}, s32[]{:S(2)}) async-start(s8[7340032]{0:T(1024)(128)(4,1)} %bitcast.79), calls=%async_computation.9 | async-start | bytes 8388608
  325.8 9.2 %slice-start.3 = ((s8[7340032]{0:T(1024)(128)(4,1)}), s8[3145728]{0:T(1024)(128)(4,1)S(1)}, s32[]{:S(2)}) async-start(s8[7340032]{0:T(1024)(128)(4,1)} %bitcast.79), calls=%async_computation.10 | async-start | bytes 6291456
  357.5 86.8 %copy-start.11 = (f32[128,2]{0,1:T(2,128)S(1)}, f32[128,2]{0,1:T(2,128)}, u32[]{:S(2)}) copy-start(f32[128,2]{0,1:T(2,128)} %param.35) | copy-start | bytes 3076
  435.3 36.3 %all-to-all-start.1 = ((bf16[8,32,4096]{2,0,1:T(8,128)(2,1)}), bf16[8,32,4096]{2,0,1:T(8,128)(2,1)}, u32[]{:S(2)}, u32[]{:S(2)}) async-start(bf16[8,32,4096]{2,0,1:T(8,128)(2,1)} %bitcast.72), calls=%async_computation.1 | async-start | bytes 4194304 | tf_op jit(solution)/shard_map/all_to_all | solution.py:164
  475.5 8.0 %copy-start.1 = (bf16[128,128]{1,0:T(8,128)(2,1)S(1)}, bf16[128,128]{1,0:T(8,128)(2,1)}, u32[]{:S(2)}) copy-start(bf16[128,128]{1,0:T(8,128)(2,1)} %param.21) | copy-start | bytes 98308
Sparse Core Ops, SparseCore 0:
  10.9 56.8 all-gather.6
  69.9 59.2 all-gather.4
  135.2 43.5 all-reduce.2
  357.7 77.6 reduce-scatter.3
where the time goes:
time: 500 us; the launch traced here: 490 us
  waiting for transfers between devices  185 us (37%)
  blocking collectives  179 us (36%)
  local copies, waits for them, and re-layouts  45.3 us (9%)
  matrix products  44.4 us (9%)
  between operations  14.4 us (3%)
  other arithmetic  13.7 us (3%)
  starting transfers between devices  8.24 us (2%)
    all_to_all x1, blocking collectives, local(): lax.all_to_all(outgoing, 'ctx', split_axis=1, concat_axis=1, tiled=True)  105 us
    unnamed x5, waiting for transfers between devices  78.5 us
    unnamed x1, blocking collectives  65.5 us
    psum x1, waiting for transfers between devices, local(): lax.psum(partial_value.astype(jnp.bfloat16), 'exp').astype(jnp.float32)  42.9 us
    all_gather x1, waiting for transfers between devices, local(): lax.all_gather(out_proj, 'ctx', axis=1, tiled=True)  36.7 us
    all_to_all x1, waiting for transfers between devices, local(): lax.all_to_all(summed, 'ctx', split_axis=1, concat_axis=1, tiled=True)  27.1 us
    unnamed x42, local copies, waits for them, and re-layouts  14.1 us
    dot_general x1, matrix products, local(): up_val = jnp.dot(flattened, up_rows, preferred_element_type=jnp.float32)  13 us
  transfers between devices with their start and end apart: 5, of which 4 were waited for; matrix products, arithmetic and copies ran while one was open for 2% of the time, Pallas kernels for 0%

commit v1 on v0

--- a/solution.py
+++ b/solution.py
@@ -161,7 +161,9 @@
         scatter_dimension=0,
         tiled=True,
     )
-    halves = lax.all_to_all(summed, "ctx", split_axis=1, concat_axis=1, tiled=True)
+    cells = jnp.split(summed, lax.axis_size("ctx"), axis=1)
+    incoming_2 = lax.all_to_all(jnp.stack(cells), "ctx", 0, 0)
+    halves = jnp.concatenate(incoming_2, axis=1)
     flattened, rank_ids = route_ranks(own_ids, experts)
     base_rows = rank_ids * n_ctx + flattened * PAIR
     fetch_rows = base_rows[:, None] + jnp.arange(PAIR, dtype=jnp.int32)[None, :]

time: 500 us -> 536 us (1.072)
  local copies, waits for them, and re-layouts: 45.3 us -> 80.1 us
    unnamed x42 -> x77, local copies, waits for them, and re-layouts: 14.1 us -> 48.3 us
where the time goes in v1:
time: 536 us; the launch traced here: 525 us
  waiting for transfers between devices  185 us (35%)
  blocking collectives  179 us (33%)
  local copies, waits for them, and re-layouts  80.1 us (15%)
  matrix products  44.4 us (8%)
  between operations  14.4 us (3%)
  other arithmetic  13.7 us (3%)
  starting transfers between devices  8.24 us (2%)
    all_to_all x1, blocking collectives, local(): lax.all_to_all(outgoing, 'ctx', split_axis=1, concat_axis=1, tiled=True)  105 us
    unnamed x5, waiting for transfers between devices  78.5 us
    unnamed x1, blocking collectives  65.5 us
    unnamed x77, local copies, waits for them, and re-layouts  48.3 us
    psum x1, waiting for transfers between devices, local(): lax.psum(partial_value.astype(jnp.bfloat16), 'exp').astype(jnp.float32)  42.9 us
    all_gather x1, waiting for transfers between devices, local(): lax.all_gather(out_proj, 'ctx', axis=1, tiled=True)  36.7 us
    all_to_all x1, waiting for transfers between devices, local(): incoming_2 = lax.all_to_all(jnp.stack(cells), 'ctx', 0, 0)  27.1 us
    dot_general x1, matrix products, local(): up_val = jnp.dot(flattened, up_rows, preferred_element_type=jnp.float32)  13 us
  transfers between devices with their start and end apart: 5, of which 4 were waited for; matrix products, arithmetic and copies ran while one was open for 2% of the time, Pallas kernels for 0%

profile of v1, /device:TPU:1, one launch (start us, length us, event | category | flops | bytes accessed | tf_op | source)
XLA Modules:
  0.0 525.1 jit_solution(3198832525738541760)
XLA Ops:
  6.5 1.0 reduce_window_sum.33
  7.7 1.1 copy.86
  8.8 0.8 exponential_bitcast_fusion
  9.6 1.1 convolution_convert_fusion.3
  10.8 0.7 all-gather.5.cloned.1.call-update
  11.6 1.2 dynamic-slice
  13.8 65.5 %all-reduce = bf16[512]{0:T(512)(128)(2,1)S(1)} all-reduce(bf16[512]{0:T(512)(128)(2,1)S(1)} %dynamic-update-slice), channel_id=2, replica_groups=mesh['ctx'=32,'exp'=4] {'ctx'}, use_global_device_ids=true, to_apply=%add | all-reduce | flops 512 | bytes 2048
  79.5 0.9 fusion.74
  80.5 1.2 while.12
  80.5 1.2 convert_add_fusion.3
  82.2 1.4 fusion.8
  84.1 8.4 %psum.14 = f32[128]{0:T(128)S(1)} all-reduce(f32[128]{0:T(128)S(1)} %multiply_reduce_fusion.2), channel_id=1, replica_groups=mesh['ctx'=32,'exp'=4] {'exp'}, use_global_device_ids=true, to_apply=%region_4.5 | all-reduce | flops 128 | bytes 1024 | tf_op jit(solution)/shard_map/psum | solution.py:117
  92.5 36.7 %all-gather.5.cloned.1.call-done = bf16[1024,4096]{1,0:T(8,128)(2,1)} async-done(((bf16[1024,128]{1,0:T(8,128)(2,1)}), bf16[1024,4096]{1,0:T(8,128)(2,1)}) %all-gather.5.cloned.1.call-update) | async-done | bytes 8388624 | tf_op jit(solution)/shard_map/all_gather | solution.py:122
  129.2 5.8 %convolution_convert_fusion.2 = bf16[128,4096]{1,0:T(8,128)(2,1)} fusion(bf16[1024,4096]{1,0:T(8,128)(2,1)} %all-gather.5.cloned.1.call-done, f32[1024]{0:T(1024)S(1)} %copy-done.14, f32[128]{0:T(128)S(1)} %add_rsqrt_fusion.1, f32[128,1024]{1,0:T(8,128)S(1)} %copy.87, bf16[128,1024]{1,0:T(8,128)(2,1)S(1)} %copy-done.8), kind=kOutput, calls=%fused_computation.10 | convolution fusion | flops 1075445760 | bytes 10228224 | tf_op jit(solution)/shard_map/dot_general | solution.py:120
  135.8 42.9 %all-reduce.3.cloned.1.call-done = bf16[128,4096]{1,0:T(8,128)(2,1)} async-done(((bf16[128,4096]{1,0:T(8,128)(2,1)}), bf16[128,4096]{1,0:T(8,128)(2,1)}) %all-reduce.3.cloned.1.call-update) | async-done | bytes 1048592 | tf_op jit(solution)/shard_map/psum | solution.py:132
  178.8 3.0 convert_add_fusion.1
  182.2 3.4 broadcast_in_dim.28
  185.6 2.7 reshape.157
  188.4 1.4 convolution_convert_fusion.1
  189.7 2.3 copy.89
  192.1 4.3 broadcast_in_dim.29
  196.3 105.0 %all_to_all.10 = bf16[32,32,4096]{2,0,1:T(8,128)(2,1)} all-to-all(bf16[32,32,4096]{2,0,1:T(8,128)(2,1)} %bitcast.195), channel_id=1, replica_groups=mesh['ctx'=32,'exp'=4] {'ctx'}, dimensions={1} | all-to-all | bytes 16777216 | tf_op jit(solution)/shard_map/all_to_all | solution.py:145
  301.4 11.3 %copy.90 = bf16[32,32,4096]{2,1,0:T(8,128)(2,1)} copy(bf16[32,32,4096]{2,0,1:T(8,128)(2,1)} %all_to_all.10) | data formatting | bytes 16777216 | tf_op jit(solution)/shard_map/all_to_all | solution.py:145
  312.7 13.0 %fusion.1 = f32[1024,896]{1,0:T(8,128)S(1)} fusion(bf16[1024,4096]{1,0:T(8,128)(2,1)} %bitcast.197, bf16[1,4096,896]{2,1,0:T(8,128)(2,1)} %param.32), kind=kOutput, calls=%fused_computation.5 | convolution fusion | flops 7516192768 | bytes 19398656 | tf_op jit(solution)/shard_map/dot_general | solution.py:148
  325.8 9.2 %multiply_convert_fusion = bf16[1024,896]{1,0:T(8,128)(2,1)S(1)} fusion(f32[1024,896]{1,0:T(8,128)S(1)} %fusion.1, bf16[1024,4096]{1,0:T(8,128)(2,1)S(1)} %bitcast.198, bf16[1,4096,896]{2,1,0:T(8,128)(2,1)S(1)} %bitcast.239), kind=kOutput, calls=%fused_computation.11 | convolution fusion | flops 7521697792 | bytes 21233664 | tf_op jit(solution)/shard_map/dot_general | solution.py:147
  335.0 11.2 %convolution_convert_fusion = bf16[1024,4096]{1,0:T(8,128)(2,1)} fusion(bf16[1024,896]{1,0:T(8,128)(2,1)S(1)} %multiply_convert_fusion, bf16[1,896,4096]{2,1,0:T(8,128)(2,1)S(1)} %bitcast.241), kind=kOutput, calls=%fused_computation.3 | convolution fusion | flops 7520387072 | bytes 17563648 | tf_op jit(solution)/shard_map/dot_general | solution.py:152
  346.2 11.3 %copy.99 = bf16[4,8,32,4096]{3,1,2,0:T(8,128)(2,1)} copy(bf16[4,8,32,4096]{3,2,1,0:T(8,128)(2,1)} %bitcast.199) | data formatting | bytes 16777216
  357.5 77.8 %reduce-scatter.4.cloned.1.call-done = bf16[8,131072]{1,0:T(8,128)(2,1)} async-done(((bf16[32,131072]{1,0:T(8,128)(2,1)}), bf16[8,131072]{1,0:T(8,128)(2,1)}) %reduce-scatter.4.cloned.1.call-update) | async-done | bytes 2097168
  435.3 1.6 fusion.65
  436.9 1.5 fusion.64
  438.4 1.5 fusion.63
  439.8 1.5 fusion.62
  441.3 1.5 fusion.61
  442.7 1.5 fusion.60
  444.2 1.5 fusion.59
  445.7 1.5 fusion.58
  447.1 1.5 fusion.57
  448.6 1.5 fusion.56
  450.1 1.5 fusion.55
  451.5 1.5 fusion.54
  453.0 1.5 fusion.53
  454.4 1.5 fusion.52
  455.9 1.5 fusion.51
  457.4 1.5 fusion.50
  458.8 0.6 fusion.49
  459.4 0.6 fusion.48
  460.7 0.6 fusion.46
  461.9 0.6 fusion.44
  462.5 0.6 fusion.43
  463.8 0.6 fusion.41
  464.4 0.6 fusion.40
  465.6 0.6 fusion.38
  466.3 0.6 fusion.37
  467.5 0.6 fusion.35
  468.1 0.6 fusion.34
  468.8 8.1 %all-to-all-start.1 = ((bf16[32,8,1,4096]{3,1,2,0:T(8,128)(2,1)}), bf16[32,8,1,4096]{3,1,2,0:T(8,128)(2,1)S(1)}, u32[]{:S(2)}, u32[]{:S(2)}) async-start(bf16[32,8,1,4096]{3,1,2,0:T(8,128)(2,1)} %fusion.34), calls=%async_computation.1 | async-start | bytes 4194304 | tf_op jit(solution)/shard_map/all_to_all | solution.py:165
  478.0 27.1 %all-to-all-done.1 = bf16[32,8,1,4096]{3,1,2,0:T(8,128)(2,1)S(1)} async-done(((bf16[32,8,1,4096]{3,1,2,0:T(8,128)(2,1)}), bf16[32,8,1,4096]{3,1,2,0:T(8,128)(2,1)S(1)}, u32[]{:S(2)}, u32[]{:S(2)}) %all-to-all-start.1) | async-done | bytes 2097184 | tf_op jit(solution)/shard_map/all_to_all | solution.py:165
  505.1 1.3 copy-done.3
  506.4 2.7 copy.92
  509.2 1.2 gather_fusion
  510.4 1.3 reshape.175
  511.7 2.7 reduce_sum.60
  515.1 1.4 multiply_reduce_fusion.1
  516.5 1.8 add_convert_fusion
  (88 shorter events, 7.8 us)
Async XLA Ops:
  6.5 3.1 copy-start
  6.5 73.8 %all-gather.7.cloned.1.call-start = ((), (), s32[]{:S(2)}) async-start(), calls=%async_computation.5 | async-start | bytes 8650752 | tf_op jit(solution)/shard_map/all_gather | solution.py:14
  10.7 118.4 %all-gather.5.cloned.1.call-start = ((), (), s32[]{:S(2)}) async-start(), calls=%async_computation.3 | async-start | bytes 8650752 | tf_op jit(solution)/shard_map/all_gather | solution.py:122
  11.5 167.3 %all-reduce.3.cloned.1.call-start = ((), (), s32[]{:S(2)}) async-start(), calls=%async_computation.4 | async-start | bytes 2097152 | tf_op jit(solution)/shard_map/psum | solution.py:132
  80.4 1.3 copy-start.7
  80.4 1.3 copy-start.9
  80.5 1.7 copy-start.11
  80.5 1.7 copy-start.15
  82.2 1.6 copy-start.8
  82.2 47.0 %copy-start.14 = (f32[1024]{0:T(1024)S(1)}, f32[1024]{0:T(1024)}, u32[]{:S(2)}) copy-start(f32[1024]{0:T(1024)} %param.27) | copy-start | bytes 12292
  92.5 42.6 %copy-start.12 = (s32[128,2]{0,1:T(2,128)S(1)}, s32[128,2]{0,1:T(2,128)}, u32[]{:S(2)}) copy-start(s32[128,2]{0,1:T(2,128)} %param.34) | copy-start | bytes 3076
  135.0 43.7 %copy-start.4 = (bf16[128,4096]{1,0:T(8,128)(2,1)S(1)}, bf16[128,4096]{1,0:T(8,128)(2,1)}, u32[]{:S(2)}) copy-start(bf16[128,4096]{1,0:T(8,128)(2,1)} %param.29) | copy-start | bytes 3145732
  135.1 300.2 %reduce-scatter.4.cloned.1.call-start = ((), (), s32[]{:S(2)}) async-start(), calls=%async_computation.6 | async-start | bytes 10485760
  135.8 45.9 %copy-start.10 = (f32[4096]{0:T(1024)S(1)}, f32[4096]{0:T(1024)}, u32[]{:S(2)}) copy-start(f32[4096]{0:T(1024)} %param.30) | copy-start | bytes 49156
  178.8 3.0 copy-start.5
  301.4 24.4 %slice-start = ((s8[7340032]{0:T(1024)(128)(4,1)}), s8[3145728]{0:T(1024)(128)(4,1)S(1)}, s32[]{:S(2)}) async-start(s8[7340032]{0:T(1024)(128)(4,1)} %bitcast.238), calls=%async_computation.7 | async-start | bytes 6291456
  312.7 13.0 %copy-start.2 = (bf16[32,32,4096]{2,1,0:T(8,128)(2,1)S(1)}, bf16[32,32,4096]{2,1,0:T(8,128)(2,1)}, u32[]{:S(2)}) copy-start(bf16[32,32,4096]{2,1,0:T(8,128)(2,1)} %copy.90) | copy-start | bytes 25165828
  312.7 13.0 %slice-start.1 = ((s8[7340032]{0:T(1024)(128)(4,1)}), s8[4194304]{0:T(1024)(128)(4,1)S(1)}, s32[]{:S(2)}) async-start(s8[7340032]{0:T(1024)(128)(4,1)} %bitcast.238), calls=%async_computation.8 | async-start | bytes 8388608
  312.7 22.2 %slice-start.2 = ((s8[7340032]{0:T(1024)(128)(4,1)}), s8[4194304]{0:T(1024)(128)(4,1)S(1)}, s32[]{:S(2)}) async-start(s8[7340032]{0:T(1024)(128)(4,1)} %bitcast.240), calls=%async_computation.9 | async-start | bytes 8388608
  325.7 9.2 %slice-start.3 = ((s8[7340032]{0:T(1024)(128)(4,1)}), s8[3145728]{0:T(1024)(128)(4,1)S(1)}, s32[]{:S(2)}) async-start(s8[7340032]{0:T(1024)(128)(4,1)} %bitcast.240), calls=%async_computation.10 | async-start | bytes 6291456
  435.3 23.5 %copy-start.6 = (bf16[8,131072]{1,0:T(8,128)(2,1)S(1)}, bf16[8,131072]{1,0:T(8,128)(2,1)}, u32[]{:S(2)}) copy-start(bf16[8,131072]{1,0:T(8,128)(2,1)} %reduce-scatter.4.cloned.1.call-done) | copy-start | bytes 6291460
  468.8 9.0 %copy-start.13 = (f32[128,2]{0,1:T(2,128)S(1)}, f32[128,2]{0,1:T(2,128)}, u32[]{:S(2)}) copy-start(f32[128,2]{0,1:T(2,128)} %param.35) | copy-start | bytes 3076
  468.8 36.3 %all-to-all-start.1 = ((bf16[32,8,1,4096]{3,1,2,0:T(8,128)(2,1)}), bf16[32,8,1,4096]{3,1,2,0:T(8,128)(2,1)S(1)}, u32[]{:S(2)}, u32[]{:S(2)}) async-start(bf16[32,8,1,4096]{3,1,2,0:T(8,128)(2,1)} %fusion.34), calls=%async_computation.1 | async-start | bytes 4194304 | tf_op jit(solution)/shard_map/all_to_all | solution.py:165
  505.1 1.4 copy-start.3
  511.7 6.6 %copy-start.1 = (bf16[128,128]{1,0:T(8,128)(2,1)S(1)}, bf16[128,128]{1,0:T(8,128)(2,1)}, u32[]{:S(2)}) copy-start(bf16[128,128]{1,0:T(8,128)(2,1)} %param.21) | copy-start | bytes 98308
Sparse Core Ops, SparseCore 0:
  10.9 56.8 all-gather.6
  69.9 59.2 all-gather.4
  135.2 43.5 all-reduce.2
  357.6 77.6 reduce-scatter.3
